TPU v7x, 512 devices: a whole 4x8x8 slice. The times are simulated.
512 devices in a mesh: dp: 16 (over z_lo, y), mp: 32 (over x, z_hi, core).
Axes of the slice: x: 4, y: 8, z: 8 (z_hi: 4, z_lo: 2; z = z_hi * 2 + z_lo), core: 2. Of those that a mesh axis runs over, the one named last changes fastest.
Arguments:
- out_grads: bfloat16 [2048, 28672], P('dp', 'mp'), may hold values from -6 to 6
- inputs: bfloat16 [2048, 8192], P('mp', 'dp'), may hold values from -6 to 6
- out_basis: bfloat16 [28672, 14336], P('mp', 'dp'), may hold values from -0.03125 to 0.03125
- in_basis: bfloat16 [8192, 8192], P('dp', 'mp'), may hold values from -0.0625 to 0.0625
- query_out: bfloat16 [128, 28672], P('dp', 'mp'), may hold values from -2.390625 to 2.390625
- query_in: bfloat16 [128, 8192], P('mp', 'dp'), may hold values from -2.390625 to 2.390625
- damping: float32 [1], replicated, may hold values from 0.5 to 2
Outputs:
- eigenvalues: float32 [14336, 8192], P('dp', 'mp')
- preconditioned: bfloat16 [4, 14336, 8192], P(None, 'dp', 'mp')
All inputs are finite; a program needn't handle non-finite values.
Results may differ from a plain program's by a relative error of at most 0.033.
Values may be sent and summed in bfloat16 or wider, within the bound.
A program may use at most 64 MiB of HBM per device.

v0:
```python
import jax
import jax.numpy as jnp
from jax import lax
from jax.sharding import PartitionSpec as P

RANK = 32


def paired_product(left, right):
    return lax.dot_general(
        left, right, (((1,), (1,)), ((0,), (0,))), preferred_element_type=jnp.float32
    )


def shards(out_grads, inputs, out_basis, in_basis, query_out, query_in, damping):
    grad_rows, left_rows = (
        lax.all_gather(out_grads, "dp", axis=0, tiled=True),
        lax.all_gather(query_out, "dp", axis=0, tiled=True),
    )
    grad_terms = jnp.dot(grad_rows, out_basis, preferred_element_type=jnp.float32)
    left_terms = jnp.dot(left_rows, out_basis, preferred_element_type=jnp.float32)
    grad_part, left_part = (
        lax.psum_scatter(
            grad_terms.astype(jnp.bfloat16), "mp", scatter_dimension=1, tiled=True
        ).astype(jnp.float32),
        lax.psum_scatter(
            left_terms.astype(jnp.bfloat16), "mp", scatter_dimension=1, tiled=True
        ).astype(jnp.float32),
    )
    rot_grads, rot_left = (
        lax.all_gather(grad_part.astype(jnp.bfloat16), "mp", axis=1, tiled=True),
        lax.all_gather(left_part.astype(jnp.bfloat16), "mp", axis=1, tiled=True),
    )
    act_rows, right_rows = (
        lax.all_gather(inputs, "mp", axis=0, tiled=True),
        lax.all_gather(query_in, "mp", axis=0, tiled=True),
    )
    act_terms = jnp.dot(act_rows, in_basis, preferred_element_type=jnp.float32)
    right_terms = jnp.dot(right_rows, in_basis, preferred_element_type=jnp.float32)
    act_total, right_total = (
        lax.psum(act_terms.astype(jnp.bfloat16), "dp").astype(jnp.float32),
        lax.psum(right_terms.astype(jnp.bfloat16), "dp").astype(jnp.float32),
    )
    rot_inputs = act_total.astype(jnp.bfloat16)
    rot_right = right_total.astype(jnp.bfloat16)
    length = rot_grads.shape[0] // 2
    rotated = paired_product(
        rot_grads.reshape(2, length, rot_grads.shape[1]),
        rot_inputs.reshape(2, length, rot_inputs.shape[1]),
    )
    eigenvalues = jnp.sum(rotated * rotated, axis=0) / (2.0 * length)
    queries = rot_left.shape[0] // RANK
    product = paired_product(
        rot_left.reshape(queries, RANK, rot_left.shape[1]),
        rot_right.reshape(queries, RANK, rot_right.shape[1]),
    )
    preconditioned = (product / (eigenvalues + damping[0])).astype(jnp.bfloat16)
    return (eigenvalues, preconditioned)


def solution(mesh):
    placed = (
        P("dp", "mp"),
        P("mp", "dp"),
        P("mp", "dp"),
        P("dp", "mp"),
        P("dp", "mp"),
        P("mp", "dp"),
        P(),
    )
    return jax.shard_map(
        shards,
        mesh=mesh,
        in_specs=placed,
        out_specs=(P("dp", "mp"), P(None, "dp", "mp")),
        check_vma=False,
    )
```

profile of v0, /device:TPU:2, one launch (start us, length us, event | category | flops | bytes accessed | tf_op | source)
XLA Modules:
  0.0 441.8 jit_solution(5737156211594645909)
XLA Ops:
  7.2 0.7 all-gather.7.cloned.1.call-update
  8.0 0.7 all-gather.9.cloned.1.call-update
  8.7 36.8 %all_gather.21 = bf16[128,896]{1,0:T(8,128)(2,1)S(1)} all-gather(bf16[8,896]{1,0:T(8,128)(2,1)} %param.11), channel_id=1, replica_groups=mesh['dp'=16,'mp'=32] {'dp'}, dimensions={0}, use_global_device_ids=true | all-gather | bytes 243712 | tf_op jit(solution)/shard_map/all_gather | solution.py:18
  45.5 0.7 convolution_convert_fusion.2
  46.2 47.0 %all-gather.7.cloned.1.call-done = bf16[2048,896]{1,0:T(8,128)(2,1)} async-done(((bf16[128,896]{1,0:T(8,128)(2,1)}), bf16[2048,896]{1,0:T(8,128)(2,1)}) %all-gather.7.cloned.1.call-update) | async-done | bytes 3670032 | tf_op jit(solution)/shard_map/all_gather | solution.py:17
  93.2 7.9 %convolution_convert_fusion = bf16[2048,896]{0,1:T(8,128)(2,1)} fusion(bf16[2048,896]{1,0:T(8,128)(2,1)} %all-gather.7.cloned.1.call-done, bf16[896,896]{1,0:T(8,128)(2,1)S(1)} %copy-done), kind=kOutput, calls=%fused_computation.1 | convolution fusion | flops 3290169344 | bytes 8945664 | tf_op jit(solution)/shard_map/dot_general | solution.py:20
  101.1 91.4 %fusion.2 = (bf16[2048,32]{0,1:T(8,128)(2,1)S(1)}, bf16[128,32]{0,1:T(8,128)(2,1)S(1)}) fusion(bf16[2048,896]{0,1:T(8,128)(2,1)} %convolution_convert_fusion, bf16[128,896]{0,1:T(8,128)(2,1)S(1)} %convolution_convert_fusion.2), kind=kCustom, calls=%all-reduce-scatter.2 | all-reduce-scatter fusion | flops 2228225 | bytes 4040704
  192.4 1.9 collective-permute-start
  194.4 1.9 collective-permute-start.1
  196.3 1.9 collective-permute-start.2
  198.3 7.3 %collective-permute-start.3 = (bf16[2048,28]{0,1:T(8,128)(2,1)S(1)}, bf16[2048,28]{0,1:T(8,128)(2,1)S(1)}, u32[]{:S(2)}, u32[]{:S(2)}) collective-permute-start(bf16[2048,28]{0,1:T(8,128)(2,1)S(1)} %slice), channel_id=1, source_target_pairs={{0,4},{1,5},{2,6},{3,7},{4,8},{5,9},{6,10},{7,11},{8,12},{9,13},{1... | collective-permute-start | bytes 344072
  205.6 1.3 dynamic-slice.6
  207.5 7.6 %collective-permute-done.3 = bf16[2048,28]{0,1:T(8,128)(2,1)S(1)} collective-permute-done((bf16[2048,28]{0,1:T(8,128)(2,1)S(1)}, bf16[2048,28]{0,1:T(8,128)(2,1)S(1)}, u32[]{:S(2)}, u32[]{:S(2)}) %collective-permute-start.3) | collective-permute-done | bytes 114720
  215.1 0.9 concatenate
  216.1 0.7 dynamic-slice_bitcast_fusion
  216.8 41.0 %all-gather.2 = bf16[32,4,512]{2,1,0:T(4,128)(2,1)S(1)} all-gather(bf16[1,4,512]{2,1,0:T(4,128)(2,1)S(1)} %bitcast.41), channel_id=1, replica_groups=mesh['dp'=16,'mp'=32] {'mp'}, dimensions={0}, use_global_device_ids=true | all-gather | bytes 135168 | tf_op jit(solution)/shard_map/all_gather | solution.py:36
  257.9 0.8 convolution_convert_fusion.3
  258.7 3.3 convolution_convert_fusion.1
  262.0 2.3 collective-permute-start.4
  264.3 1.9 collective-permute-start.5
  266.2 2.2 collective-permute-start.6
  268.5 6.5 %collective-permute-start.7 = (bf16[128,28]{0,1:T(8,128)(2,1)S(1)}, bf16[128,28]{0,1:T(8,128)(2,1)S(1)}, u32[]{:S(2)}, u32[]{:S(2)}) collective-permute-start(bf16[128,28]{0,1:T(8,128)(2,1)S(1)} %slice.1), channel_id=1, source_target_pairs={{0,4},{1,5},{2,6},{3,7},{4,8},{5,9},{6,10},{7,11},{8,12},{9,13},{1... | collective-permute-start | bytes 21512
  275.6 4.0 collective-permute-done.7
  279.6 0.6 concatenate.1
  280.2 39.2 %all-gather.1 = bf16[32,28,128]{2,1,0:T(8,128)(2,1)S(1)} all-gather(bf16[1,28,128]{2,1,0:T(8,128)(2,1)S(1)} %dynamic-slice_bitcast_fusion.1), channel_id=1, replica_groups=mesh['dp'=16,'mp'=32] {'mp'}, dimensions={0}, use_global_device_ids=true | all-gather | bytes 236544 | tf_op jit(solution)/shard_map/all_gather | solution.py:32
  319.4 0.2 copy.15
  319.6 5.9 %reshape.25 = bf16[896,2048]{1,0:T(8,128)(2,1)} reshape(bf16[32,28,2048]{2,1,0:T(8,128)(2,1)} %all-gather.11.cloned.1.call-done) | data formatting | bytes 7340032
  325.5 6.1 %copy.13 = bf16[2048,896]{1,0:T(8,128)(2,1)} copy(bf16[2048,896]{0,1:T(8,128)(2,1)} %bitcast.35) | data formatting | bytes 7340032
  331.5 96.8 %all-reduce.8.cloned.1.call-done = (bf16[2,1024,256]{2,1,0:T(8,128)(2,1)}, bf16[4,32,256]{2,1,0:T(8,128)(2,1)}) async-done(((bf16[2,1024,256]{2,1,0:T(8,128)(2,1)}, bf16[4,32,256]{2,1,0:T(8,128)(2,1)}), (bf16[2,1024,256]{2,1,0:T(8,128)(2,1)}, bf16[4,32,256]{2,1,0:T(8,128)(2,1)})) %all-reduce.8.cloned.1.call-update) | async-done | bytes 1114128 | tf_op jit(solution)/shard_map/psum | solution.py:41
  428.3 3.9 multiply_reduce_fusion
  432.3 1.0 broadcast_add_fusion
  433.3 1.9 divide_convert_fusion
  (27 shorter events, 0.4 us)
Async XLA Ops:
  7.2 38.3 %copy-start = (bf16[896,896]{1,0:T(8,128)(2,1)S(1)}, bf16[896,896]{1,0:T(8,128)(2,1)}, u32[]{:S(2)}) copy-start(bf16[896,896]{1,0:T(8,128)(2,1)} %param.9) | copy-start | bytes 4816900
  7.2 86.0 %all-gather.7.cloned.1.call-start = ((), (), s32[]{:S(2)}) async-start(), calls=%async_computation | async-start | bytes 3899392 | tf_op jit(solution)/shard_map/all_gather | solution.py:17
  7.9 250.8 %all-gather.9.cloned.1.call-start = ((), (), s32[]{:S(2)}) async-start(), calls=%async_computation.1 | async-start | bytes 2162688 | tf_op jit(solution)/shard_map/all_gather | solution.py:35
  8.7 310.9 %all-gather.11.cloned.1.call-start = ((), (), s32[]{:S(2)}) async-start(), calls=%async_computation.2 | async-start | bytes 4325376 | tf_op jit(solution)/shard_map/all_gather | solution.py:31
  101.1 115.8 %copy-start.2 = (bf16[4,512]{1,0:T(4,128)(2,1)S(1)}, bf16[4,512]{1,0:T(4,128)(2,1)}, u32[]{:S(2)}) copy-start(bf16[4,512]{1,0:T(4,128)(2,1)} %param.12) | copy-start | bytes 12292
  101.1 156.8 %copy-start.1 = (bf16[512,256]{1,0:T(8,128)(2,1)S(1)}, bf16[512,256]{1,0:T(8,128)(2,1)}, u32[]{:S(2)}) copy-start(bf16[512,256]{1,0:T(8,128)(2,1)} %param.10) | copy-start | bytes 786436
  192.4 22.7 %collective-permute-start = (bf16[2048,32]{0,1:T(8,128)(2,1)S(1)}, bf16[2048,32]{0,1:T(8,128)(2,1)S(1)}, u32[]{:S(2)}, u32[]{:S(2)}) collective-permute-start(bf16[2048,32]{0,1:T(8,128)(2,1)S(1)} %get-tuple-element.6), channel_id=1, source_target_pairs={{0,1},{1,2},{2,3},{3,4},{4,5},{5,6},{6,7},{7,8},{8,9},{9,10},{10,1... | collective-permute-start | bytes 393224
  194.4 20.8 %collective-permute-start.1 = (bf16[2048,32]{0,1:T(8,128)(2,1)S(1)}, bf16[2048,32]{0,1:T(8,128)(2,1)S(1)}, u32[]{:S(2)}, u32[]{:S(2)}) collective-permute-start(bf16[2048,32]{0,1:T(8,128)(2,1)S(1)} %get-tuple-element.6), channel_id=1, source_target_pairs={{0,2},{1,3},{2,4},{3,5},{4,6},{5,7},{6,8},{7,9},{8,10},{9,11},{10,... | collective-permute-start | bytes 393224
  196.3 18.8 %collective-permute-start.2 = (bf16[2048,32]{0,1:T(8,128)(2,1)S(1)}, bf16[2048,32]{0,1:T(8,128)(2,1)S(1)}, u32[]{:S(2)}, u32[]{:S(2)}) collective-permute-start(bf16[2048,32]{0,1:T(8,128)(2,1)S(1)} %get-tuple-element.6), channel_id=1, source_target_pairs={{0,3},{1,4},{2,5},{3,6},{4,7},{5,8},{6,9},{7,10},{8,11},{9,12},{10... | collective-permute-start | bytes 393224
  198.3 16.9 %collective-permute-start.3 = (bf16[2048,28]{0,1:T(8,128)(2,1)S(1)}, bf16[2048,28]{0,1:T(8,128)(2,1)S(1)}, u32[]{:S(2)}, u32[]{:S(2)}) collective-permute-start(bf16[2048,28]{0,1:T(8,128)(2,1)S(1)} %slice), channel_id=1, source_target_pairs={{0,4},{1,5},{2,6},{3,7},{4,8},{5,9},{6,10},{7,11},{8,12},{9,13},{1... | collective-permute-start | bytes 344072
  216.8 211.6 %all-reduce.8.cloned.1.call-start = ((), (), s32[]{:S(2)}) async-start(), calls=%async_computation.3 | async-start | bytes 2228224 | tf_op jit(solution)/shard_map/psum | solution.py:41
  262.0 17.6 %collective-permute-start.4 = (bf16[128,32]{0,1:T(8,128)(2,1)S(1)}, bf16[128,32]{0,1:T(8,128)(2,1)S(1)}, u32[]{:S(2)}, u32[]{:S(2)}) collective-permute-start(bf16[128,32]{0,1:T(8,128)(2,1)S(1)} %get-tuple-element.7), channel_id=1, source_target_pairs={{0,1},{1,2},{2,3},{3,4},{4,5},{5,6},{6,7},{7,8},{8,9},{9,10},{10,1... | collective-permute-start | bytes 24584
  264.3 15.3 %collective-permute-start.5 = (bf16[128,32]{0,1:T(8,128)(2,1)S(1)}, bf16[128,32]{0,1:T(8,128)(2,1)S(1)}, u32[]{:S(2)}, u32[]{:S(2)}) collective-permute-start(bf16[128,32]{0,1:T(8,128)(2,1)S(1)} %get-tuple-element.7), channel_id=1, source_target_pairs={{0,2},{1,3},{2,4},{3,5},{4,6},{5,7},{6,8},{7,9},{8,10},{9,11},{10,... | collective-permute-start | bytes 24584
  266.2 13.4 %collective-permute-start.6 = (bf16[128,32]{0,1:T(8,128)(2,1)S(1)}, bf16[128,32]{0,1:T(8,128)(2,1)S(1)}, u32[]{:S(2)}, u32[]{:S(2)}) collective-permute-start(bf16[128,32]{0,1:T(8,128)(2,1)S(1)} %get-tuple-element.7), channel_id=1, source_target_pairs={{0,3},{1,4},{2,5},{3,6},{4,7},{5,8},{6,9},{7,10},{8,11},{9,12},{10... | collective-permute-start | bytes 24584
  268.5 11.1 %collective-permute-start.7 = (bf16[128,28]{0,1:T(8,128)(2,1)S(1)}, bf16[128,28]{0,1:T(8,128)(2,1)S(1)}, u32[]{:S(2)}, u32[]{:S(2)}) collective-permute-start(bf16[128,28]{0,1:T(8,128)(2,1)S(1)} %slice.1), channel_id=1, source_target_pairs={{0,4},{1,5},{2,6},{3,7},{4,8},{5,9},{6,10},{7,11},{8,12},{9,13},{1... | collective-permute-start | bytes 21512
  428.3 5.0 %copy-start.3 = (bf16[4,32,256]{2,1,0:T(8,128)(2,1)S(1)}, bf16[4,32,256]{2,1,0:T(8,128)(2,1)}, u32[]{:S(2)}) copy-start(bf16[4,32,256]{2,1,0:T(8,128)(2,1)} %get-tuple-element.3) | copy-start | bytes 196612
Sparse Core Ops, SparseCore 0:
  10.1 83.0 all-gather.6
  96.3 62.1 all-gather.8
  216.9 66.4 all-gather.10
  286.9 141.4 all-reduce.7
where the time goes:
time: 443 us; the launch traced here: 442 us
  blocking collectives  208 us (47%)
  waiting for transfers between devices  157 us (35%)
  starting transfers between devices  26.1 us (6%)
  matrix products  18.6 us (4%)
  local copies, waits for them, and re-layouts  15.7 us (4%)
  between operations  15.2 us (3%)
    psum x1, waiting for transfers between devices, shards(): lax.psum(act_terms.astype(jnp.bfloat16), 'dp').astype(jnp.float32)  96.8 us
    unnamed x1, blocking collectives  91.4 us
    all_gather x1, waiting for transfers between devices, shards(): lax.all_gather(out_grads, 'dp', axis=0, tiled=True)  47 us
    all_gather x1, blocking collectives, shards(): lax.all_gather(query_in, 'mp', axis=0, tiled=True)  41 us
    all_gather x1, blocking collectives, shards(): lax.all_gather(left_part.astype(jnp.bfloat16), 'mp', axis=1, tiled=True)  39.2 us
    all_gather x1, blocking collectives, shards(): lax.all_gather(query_out, 'dp', axis=0, tiled=True)  36.8 us
    unnamed x8, starting transfers between devices  26 us
    unnamed x20, local copies, waits for them, and re-layouts  15.7 us
  transfers between devices with their start and end apart: 12, of which 4 were waited for; matrix products, arithmetic and copies ran while one was open for 27% of the time, Pallas kernels for 0%

commit v1 on v0

v1 whole, which is shorter than its diff:
```python
import jax
import jax.numpy as jnp
from jax import lax
from jax.experimental import pallas as pl
from jax.experimental.pallas import tpu as pltpu
from jax.sharding import PartitionSpec as P

BF = jnp.bfloat16
F32 = jnp.float32
MESH = pl.DeviceIdType.MESH
NT = (((1,), (1,)), ((), ()))

NY, NX, NH = 8, 4, 4
CHUNKS = ((0, 1), (1, 2), (3, 2), (5, 2), (7, 1))
QSLOT = 8
OFFSETS = (0, -1, 1, -2, 2, -3, 3, 4)
UP = {0: 1, 1: 3, 3: 5, 5: 7}
DOWN = {0: 2, 2: 4, 4: 6, 6: 7}
N_SEND, N_RECV = 180, 180


def kernel(
    g, q, b, xc, bi, damp, eig, pre,
    gk, qk, bt, bi2, pt, r1, s1, r2, rg,
    xk, px, rzx, sx, ryx, ox, rx, xf,
    ssem, rsem,
):
    dp, mp = lax.axis_index("dp"), lax.axis_index("mp")
    a, y = lax.div(dp, NY), lax.rem(dp, NY)
    x, h, c = lax.div(mp, 8), lax.rem(lax.div(mp, 2), NH), lax.rem(mp, 2)

    def dev(a=a, y=y, x=x, h=h, c=c):
        return {"dp": a * NY + y, "mp": (x * NH + h) * 2 + c}

    def wrap(v, n):
        return lax.rem(v + n, n)

    yd = [y] + [wrap(y + d, NY) for d in range(1, NY)]
    xd = [x] + [wrap(x + d, NX) for d in range(1, NX)]
    hd = [h] + [wrap(h + d, NH) for d in range(1, NH)]
    counts = [0, 0]
    sent = []

    def new_send():
        counts[0] += 1
        assert counts[0] <= N_SEND
        return ssem.at[counts[0] - 1]

    def new_recv(n=1):
        counts[1] += n
        assert counts[1] <= N_RECV
        return counts[1] - n

    def push(src, dst, to, recv, landing=None):
        copy = pltpu.make_async_remote_copy(
            src_ref=src, dst_ref=dst, send_sem=new_send(), recv_sem=recv,
            device_id=to, device_id_type=MESH,
        )
        copy.start()
        sent.append(copy)
        return arrival(dst if landing is None else landing, recv)

    def arrival(landing, recv):
        return pltpu.make_async_copy(landing, landing, recv)

    barrier = pltpu.get_barrier_semaphore()
    partners = [dev(c=1 - c), dev(a=1 - a), dev(a=1 - a, c=1 - c)]
    partners += [dev(x=xd[d]) for d in (1, 3, 2)]
    partners += [dev(h=hd[d]) for d in (1, 3, 2)]
    partners += [dev(y=yd[d], c=cc) for d in (1, 7, 2, 6, 3, 5, 4) for cc in (c, 1 - c)]
    for to in partners:
        pl.semaphore_signal(barrier, inc=1, device_id=to, device_id_type=MESH)
    pl.semaphore_wait(barrier, len(partners))

    g0 = new_recv(2)
    q0 = new_recv(2)
    own_send = [new_send() for _ in range(2)]
    own_q = qk.at[c, a * NY + y]

    def to_other_core():
        return (
            pltpu.make_async_remote_copy(
                src_ref=g, dst_ref=gk.at[0, c], send_sem=own_send[0],
                recv_sem=rsem.at[g0 + c], device_id=dev(c=1 - c), device_id_type=MESH,
            ),
            pltpu.make_async_remote_copy(
                src_ref=q, dst_ref=own_q, send_sem=own_send[1],
                recv_sem=rsem.at[q0 + c], device_id=dev(c=1 - c), device_id_type=MESH,
            ),
        )

    @pl.when(c == a)
    def _():
        pltpu.make_async_copy(g, gk.at[0, c], rsem.at[g0 + c]).start()
        pltpu.make_async_copy(q, own_q, rsem.at[q0 + c]).start()

    @pl.when(c != a)
    def _():
        for copy in to_other_core():
            copy.start()

    push(g, gk.at[0, c], dev(a=1 - a, c=a), rsem.at[g0 + c])
    push(q, own_q, dev(a=1 - a, c=a), rsem.at[q0 + c])

    here = xk.at[x * NH + h]
    local = pltpu.make_async_copy(xc, here, rsem.at[new_recv()])
    local.start()
    x_h = []
    for d in (1, 3, 2):
        x_h.append(
            push(xc, here, dev(h=hd[d]), rsem.at[new_recv()], xk.at[x * NH + hd[NH - d]])
        )
    bi_local = pltpu.make_async_copy(bi, bi2.at[c], rsem.at[new_recv()])
    bi_local.start()
    bi_other = push(bi, bi2.at[c], dev(c=1 - c), rsem.at[new_recv()], bi2.at[1 - c])

    eye = (
        lax.broadcasted_iota(jnp.int32, (128, 128), 0)
        == lax.broadcasted_iota(jnp.int32, (128, 128), 1)
    ).astype(F32).astype(BF)

    for j in range(7):
        block = lax.dot_general(
            eye, b[:, j * 128 : (j + 1) * 128], NT, preferred_element_type=F32
        )
        bt[c, j * 128 : (j + 1) * 128, :] = block.astype(BF)
    bt_other = push(bt.at[c], bt.at[c], dev(c=1 - c), rsem.at[new_recv()], bt.at[1 - c])
    qk[:, pl.ds((1 - c) * NY, NY)] = jnp.zeros((2, NY, 8, 896), BF)

    ring = {}
    ring_recv = {(s, cb): new_recv() for s in range(1, 8) for cb in range(2)}

    def forward(slot, cb):
        for table, to in ((UP, 1), (DOWN, 7)):
            dst = table.get(slot)
            if dst is None or (dst == 7 and cb != (0 if table is UP else 1)):
                continue
            ring[dst, cb] = push(
                gk.at[slot, cb], gk.at[dst, cb], dev(y=yd[to]), rsem.at[ring_recv[dst, cb]]
            )

    for cb in range(2):
        arrival(gk.at[0, cb], rsem.at[g0 + cb]).wait()
        forward(0, cb)

    local.wait()
    for one in x_h:
        one.wait()
    x_x = []
    for d in (1, 3, 2):
        x_x.append(
            push(
                xk.at[pl.ds(x * NH, NH)], xk.at[pl.ds(x * NH, NH)], dev(x=xd[d]),
                rsem.at[new_recv()], xk.at[pl.ds(xd[NX - d] * NH, NH)],
            )
        )

    for cb in range(2):
        arrival(qk.at[cb, c * NY + y], rsem.at[q0 + cb]).wait()
    q_y = []
    for d in (1, 7, 2, 6, 3, 5, 4):
        q_y.append(
            push(
                qk.at[:, c * NY + y], qk.at[:, c * NY + y], dev(y=yd[d]),
                rsem.at[new_recv()], qk.at[:, c * NY + yd[NY - d]],
            )
        )

    def x_piece(d, recv):
        at = xd[(NX - d) % NX]
        rows = xk[pl.ds(at * NH, NH)].reshape(NH * 72, 512)
        for jc in range(2):
            part = jnp.dot(rows, bi2[jc], preferred_element_type=F32)
            part = part.astype(BF).reshape(2, 2, 72, 256)
            px[at, :, :, jc] = part
        return push(px.at[at, :, 1 - a], rzx.at[at], dev(a=1 - a), rsem.at[recv])

    x_z_recv = new_recv(NX)
    bi_local.wait()
    bi_other.wait()
    x_z = {}
    x_z[0] = x_piece(0, x_z_recv + x)

    def product(lhs_rows, s0, ns):
        def body(i, _):
            total = None
            for cb in range(2):
                left = bt[cb, pl.ds(pl.multiple_of(i * 224, 8), 224), :]
                part = lax.dot_general(left, lhs_rows[cb], NT, preferred_element_type=F32)
                total = part if total is None else total + part
            for k in range(ns):
                tile = total[:, k * 128 : (k + 1) * 128].reshape(NH, 56, 128)
                pt[s0 + k, pl.ds(i * NH, NH)] = tile.astype(BF)
            return 0

        lax.fori_loop(0, NX, body, 0)

    state = {}

    def send_x(s0, ns):
        state[s0, "x"] = [
            push(
                pt.at[pl.ds(s0, ns), pl.ds(xd[d] * NH, NH)], r1.at[d - 1, pl.ds(s0, ns)],
                dev(x=xd[d]), rsem.at[new_recv()],
            )
            for d in (1, 3, 2)
        ]

    def b1(k):
        s0, ns = CHUNKS[k]
        for s in range(s0, s0 + ns):
            for cb in range(2):
                if s > 0:
                    ring[s, cb].wait()
                    forward(s, cb)
        rows = [gk[s0 : s0 + ns, cb].reshape(ns * 128, 896) for cb in range(2)]
        product(rows, s0, ns)
        send_x(s0, ns)

    def b1q():
        for one in q_y:
            one.wait()
        rows = [qk[cb].astype(F32).reshape(128, 896).astype(BF) for cb in range(2)]
        product(rows, QSLOT, 1)
        send_x(QSLOT, 1)

    def spans(k):
        return (QSLOT, 1) if k == "q" else CHUNKS[k]

    def b2(k):
        s0, ns = spans(k)
        for one in state[s0, "x"]:
            one.wait()
        for s in range(s0, s0 + ns):
            total = pt[s, pl.ds(x * NH, NH)].astype(F32)
            for d in range(3):
                total += r1[d, s].astype(F32)
            s1[s] = total.astype(BF)
        state[s0, "z"] = [
            push(
                s1.at[pl.ds(s0, ns), hd[d]], r2.at[d - 1, pl.ds(s0, ns)],
                dev(h=hd[d]), rsem.at[new_recv()],
            )
            for d in (1, 3, 2)
        ]

    def b3(k):
        s0, ns = spans(k)
        for one in state[s0, "z"]:
            one.wait()
        for s in range(s0, s0 + ns):
            total = s1[s, h].astype(F32)
            for d in range(3):
                total += r2[d, s].astype(F32)
            rg[c, s, x * NH + h] = total.astype(BF)
        mine = rg.at[c, pl.ds(s0, ns), x * NH + h]
        state[s0, "gz"] = [
            push(
                mine, mine, dev(h=hd[d]), rsem.at[new_recv()],
                rg.at[c, pl.ds(s0, ns), x * NH + hd[NH - d]],
            )
            for d in (1, 3, 2)
        ]

    def c2(k):
        s0, ns = spans(k)
        for one in state[s0, "gz"]:
            one.wait()
        mine = rg.at[c, pl.ds(s0, ns), pl.ds(x * NH, NH)]
        state[s0, "gx"] = [
            push(
                mine, mine, dev(x=xd[d]), rsem.at[new_recv()],
                rg.at[c, pl.ds(s0, ns), pl.ds(xd[NX - d] * NH, NH)],
            )
            for d in (1, 3, 2)
        ]

    def c3(k):
        s0, ns = spans(k)
        for one in state[s0, "gx"]:
            one.wait()
        state[s0, "core"] = push(
            rg.at[c, pl.ds(s0, ns)], rg.at[c, pl.ds(s0, ns)], dev(c=1 - c),
            rsem.at[new_recv()], rg.at[1 - c, pl.ds(s0, ns)],
        )

    bt_other.wait()
    b1(0)
    b1q()
    b1(1)
    b2(0)
    b2("q")

    for i, d in enumerate((1, 3, 2)):
        x_x[i].wait()
        x_z[d] = x_piece(d, x_z_recv + xd[NX - d])
    for d in (0, 1, 3, 2):
        at = xd[(NX - d) % NX]
        x_z[d].wait()
        total = px[at, :, a].astype(F32) + rzx[at].astype(F32)
        sx[pl.ds(at * 2, 2)] = total.astype(BF)
    x_y = []
    for d in (1, 7, 2, 6, 3, 5, 4):
        x_y.append(push(sx.at[yd[d]], ryx.at[d - 1], dev(y=yd[d]), rsem.at[new_recv()]))

    b3(0)
    b3("q")
    b1(2)
    b2(1)
    c2(0)
    c2("q")

    for one in x_y:
        one.wait()
    total = sx[y].astype(F32)
    for d in range(7):
        total += ryx[d].astype(F32)
    ox[...] = total.astype(BF)
    rx_recv = new_recv(16)
    rx[c, y, a] = ox[c]
    push(ox.at[1 - c], rx.at[c, y, a], dev(c=1 - c), rsem.at[rx_recv], rx.at[1 - c, y, a])
    rx_in = [arrival(rx.at[1 - c, y, a], rsem.at[rx_recv])]
    for d in (1, 7, 2, 6, 3, 5, 4):
        for same in range(2):
            jc = c if same == 0 else 1 - c
            recv = rsem.at[rx_recv + 1 + (d - 1) * 2 + same]
            push(ox.at[jc], rx.at[c, y, a], dev(y=yd[d], c=jc), recv)
            rx_in.append(arrival(rx.at[jc, yd[NY - d], a], recv))

    b3(1)
    c3(0)
    c3("q")
    b1(3)
    b2(2)
    c2(1)

    for one in rx_in:
        one.wait()
    rx_z = []
    for ch in range(2):
        rx_z.append(
            push(
                rx.at[ch, :, a], rx.at[ch, :, a], dev(a=1 - a),
                rsem.at[new_recv()], rx.at[ch, :, 1 - a],
            )
        )

    b3(2)
    c3(1)
    b1(4)
    b2(3)
    c2(2)
    b3(3)
    b2(4)
    c3(2)
    c2(3)
    b3(4)
    for one in rx_z:
        one.wait()
    for n in range(2):
        for s in range(8):
            shard = n * NY + wrap(y + OFFSETS[s], NY)
            for ch in range(2):
                at = s * 128 + ch * 64
                xf[n, at : at + 64] = rx[ch, lax.div(shard, 2), lax.rem(shard, 2), 0:64]
    c3(3)
    c2(4)
    c3(4)
    for k in (0, 1, 2, 3, 4, "q"):
        state[spans(k)[0], "core"].wait()

    right = rx[0, :, :, 64:72].astype(F32) + rx[1, :, :, 64:72].astype(F32)
    right = right.reshape(128, 256)
    row_query = lax.broadcasted_iota(jnp.int32, (128, 256), 0) // 32
    right = jnp.concatenate(
        [jnp.where(row_query == k, right, 0.0).astype(BF) for k in range(4)], axis=1
    )

    def finish(i, _):
        piece = pl.ds(i * NH, NH)
        squares = None
        for n in range(2):
            left = jnp.concatenate(
                [rg[n, s, piece].reshape(224, 128) for s in range(8)], axis=1
            )
            rotated = jnp.dot(left, xf[n], preferred_element_type=F32)
            squares = rotated * rotated if squares is None else squares + rotated * rotated
        values = squares * (1.0 / 2048.0)
        rows = pl.ds(pl.multiple_of(i * 224, 8), 224)
        eig[rows] = values
        scale = 1.0 / (values + damp[0])
        left = (rg[0, QSLOT, piece] + rg[1, QSLOT, piece]).reshape(224, 128)
        products = jnp.dot(left, right, preferred_element_type=F32)
        for k in range(4):
            pre[k, rows] = (products[:, k * 256 : (k + 1) * 256] * scale).astype(BF)
        return 0

    lax.fori_loop(0, NX, finish, 0)

    @pl.when(c != a)
    def _():
        for copy in to_other_core():
            copy.wait_send()

    for copy in sent:
        copy.wait_send()


def shards(out_grads, inputs, out_basis, in_basis, query_out, query_in, damping):
    c = lax.rem(lax.axis_index("mp"), 2)
    zero = jnp.zeros_like(query_in)
    packed = jnp.concatenate(
        [
            inputs,
            jnp.where(c == 0, query_in, zero),
            jnp.where(c == 1, query_in, zero),
        ],
        axis=0,
    )
    vmem = pl.BlockSpec(memory_space=pltpu.VMEM)
    return pl.pallas_call(
        kernel,
        out_shape=(
            jax.ShapeDtypeStruct((896, 256), F32),
            jax.ShapeDtypeStruct((4, 896, 256), BF),
        ),
        in_specs=[vmem] * 5 + [pl.BlockSpec(memory_space=pltpu.SMEM)],
        out_specs=(vmem, vmem),
        scratch_shapes=[
            pltpu.VMEM((8, 2, 128, 896), BF),
            pltpu.VMEM((2, 16, 8, 896), BF),
            pltpu.VMEM((2, 896, 896), BF),
            pltpu.VMEM((2, 512, 256), BF),
            pltpu.VMEM((9, 16, 56, 128), BF),
            pltpu.VMEM((3, 9, 4, 56, 128), BF),
            pltpu.VMEM((9, 4, 56, 128), BF),
            pltpu.VMEM((3, 9, 56, 128), BF),
            pltpu.VMEM((2, 9, 16, 56, 128), BF),
            pltpu.VMEM((16, 72, 512), BF),
            pltpu.VMEM((4, 2, 2, 2, 72, 256), BF),
            pltpu.VMEM((4, 2, 2, 72, 256), BF),
            pltpu.VMEM((8, 2, 72, 256), BF),
            pltpu.VMEM((7, 2, 72, 256), BF),
            pltpu.VMEM((2, 72, 256), BF),
            pltpu.VMEM((2, 8, 2, 72, 256), BF),
            pltpu.VMEM((2, 1024, 256), BF),
            pltpu.SemaphoreType.DMA((N_SEND,)),
            pltpu.SemaphoreType.DMA((N_RECV,)),
        ],
        compiler_params=pltpu.CompilerParams(
            collective_id=0, has_side_effects=True, vmem_limit_bytes=60 * 1024 * 1024
        ),
    )(out_grads, query_out, out_basis, packed, in_basis, damping)


def solution(mesh):
    placed = (
        P("dp", "mp"),
        P("mp", "dp"),
        P("mp", "dp"),
        P("dp", "mp"),
        P("dp", "mp"),
        P("mp", "dp"),
        P(),
    )
    return jax.shard_map(
        shards,
        mesh=mesh,
        in_specs=placed,
        out_specs=(P("dp", "mp"), P(None, "dp", "mp")),
        check_vma=False,
    )
```

time: 443 us -> 157 us (0.35)
  the two profiles are of different devices: /device:TPU:2 before, /device:TPU:1 now
where the time goes in v1:
time: 157 us
  Pallas kernels  150 us (96%)
  local copies, waits for them, and re-layouts  3.53 us (2%)
  other arithmetic  2.18 us (1%)
    pallas_call x1, Pallas kernels, shards(): pl.pallas_call(kernel, out_shape=(jax.ShapeDtypeStruct((896, 256), F32),...  150 us
    unnamed x4, local copies, waits for them, and re-layouts  3.53 us

profile of v1, /device:TPU:1, one launch (start us, length us, event | category | flops | bytes accessed | tf_op | source)
XLA Modules:
  0.0 157.2 jit_solution(2278184442633916618)
XLA Ops:
  1.3 0.7 broadcast_select_fusion.1
  2.0 1.5 pad_maximum_fusion.xc
  3.5 150.2 %shard_map.86 = (f32[896,256]{1,0:T(8,128)}, bf16[4,896,256]{2,1,0:T(8,128)(2,1)}) custom-call(bf16[128,896]{1,0:T(8,128)(2,1)} %g.1, bf16[8,896]{1,0:T(8,128)(2,1)} %q.1, bf16[896,896]{1,0:T(8,128)(2,1)} %b.1, bf16[72,512]{1,0:T(8,128)(2,1)} %pad_maximum_fusion.xc, bf16[512,256]{1,0:T(8,128)(2,1)} %bi.1, f32[1]{0:T(128)S(6)} %copy.11.damp), custom_call_target="tpu_custom_call" | custom-call | tf_op jit(solution)/shard_map/pallas_call | solution.py:421
  153.7 0.0 copy-start
  153.7 2.3 %copy.12 = f32[896,256]{1,0:T(8,128)} copy(f32[896,256]{1,0:T(8,128)} %get-tuple-element.6) | data formatting | bytes 1835008
  156.0 0.0 copy-done
  156.0 1.2 copy.13
Async XLA Ops:
  153.7 2.3 %copy-start = (bf16[4,896,256]{2,1,0:T(8,128)(2,1)S(1)}, bf16[4,896,256]{2,1,0:T(8,128)(2,1)}, u32[]{:S(2)}) copy-start(bf16[4,896,256]{2,1,0:T(8,128)(2,1)} %get-tuple-element.7) | copy-start | bytes 5505028

commit v2 on v0

v2 whole, which is shorter than its diff:
```python
import jax
import jax.numpy as jnp
from jax import lax
from jax.experimental import pallas as pl
from jax.experimental.pallas import tpu as pltpu
from jax.sharding import PartitionSpec as P

BF = jnp.bfloat16
F32 = jnp.float32
MESH = pl.DeviceIdType.MESH
NT = (((1,), (1,)), ((), ()))

NY, NX, NH = 8, 4, 4
CHUNKS = ((0, 1), (1, 2), (3, 2), (5, 2), (7, 1))
QSLOT = 8
OFFSETS = (0, -1, 1, -2, 2, -3, 3, 4)
UP = {0: 1, 1: 3, 3: 5, 5: 7}
DOWN = {0: 2, 2: 4, 4: 6, 6: 7}
N_SEND, N_RECV = 23, 113

ORDER = (
    "x0", "g0", "bt", "rb0", "h1", "q0", "ra12", "b1_0", "h2", "rb12", "q12", "h3", "bi", "bx_0", "b1_1",
    "ra34", "bx_1", "xs1", "rb34", "q34", "by_0", "b1_2", "by_1", "xs2", "xs3", "b2_0", "bx_2", "ra56", "b2_1",
    "rb56", "q56", "xm", "b1_3", "b3_0", "by_2", "b3_1", "bx_3", "r7", "xy", "b1_4", "q7", "b1_q", "c2_0",
    "b2_2", "by_3", "bx_4", "bx_q", "c2_1", "cy_0", "b3_2", "b2_3", "by_4", "by_q", "c3_0", "cy_1", "c2_2",
    "b2_4", "b2_q", "xo", "b3_3", "c3_1", "b3_4", "b3_q", "cy_2", "xz17", "c2_3", "xz26", "c2_4", "c2_q",
    "c3_2", "cy_3", "xz354", "cy_4", "cy_q", "c3_3", "c3_4", "c3_q", "c4_0", "c4_1", "c4_2", "xf", "fin",
    "c4_3", "c4_4", "c4_q",
)


def kernel(
    g, q, b, xi, qi, bi, rg_out, xf_out, right_out,
    gk, qk, bv, bt, bix, pf, ps, pr, pt, rf, pa, r1, s1, r2, rg,
    xc, xk, sx, ryx, rx, xf, right_v,
    ssem, rsem,
):
    dp, mp = lax.axis_index("dp"), lax.axis_index("mp")
    a, y = lax.div(dp, NY), lax.rem(dp, NY)
    x, h, c = lax.div(mp, 8), lax.rem(lax.div(mp, 2), NH), lax.rem(mp, 2)
    m = x * NH + h

    def dev(a=a, y=y, x=x, h=h, c=c):
        return {"dp": a * NY + y, "mp": (x * NH + h) * 2 + c}

    def wrap(v, n):
        return lax.rem(v + n, n)

    yd = [y] + [wrap(y + d, NY) for d in range(1, NY)]
    xd = [x] + [wrap(x + d, NX) for d in range(1, NX)]
    hd = [h] + [wrap(h + d, NH) for d in range(1, NH)]
    counts = [0, 0]
    state = {}
    outs = []

    sends = {}

    def send_sem(kind):
        if kind not in sends:
            assert len(sends) < N_SEND
            sends[kind] = len(sends)
        return ssem.at[sends[kind]]

    def new_recv(n=1):
        counts[1] += n
        assert counts[1] <= N_RECV, counts
        return counts[1] - n

    def arrival(landing, recv):
        return pltpu.make_async_copy(landing, landing, recv)

    def push(kind, src, dst, to, landing, recv=None):
        recv = rsem.at[new_recv()] if recv is None else recv
        pltpu.make_async_remote_copy(
            src_ref=src, dst_ref=dst, send_sem=send_sem(kind), recv_sem=recv,
            device_id=to, device_id_type=MESH,
        ).start()
        return (landing, recv)

    def wait(key):
        for landing, recv in state.pop(key):
            arrival(landing, recv).wait()

    out_recv = new_recv(3)
    load_b = pltpu.make_async_copy(b, bv, rsem.at[new_recv()])
    load_b.start()
    load_bi = pltpu.make_async_copy(bi, bix.at[a], rsem.at[new_recv()])
    load_bi.start()
    factors = qi[...].astype(F32)
    factors = jnp.concatenate([factors, factors], axis=0)
    row_core = lax.broadcasted_iota(jnp.int32, (8, 512), 0) // 4
    xc[0:64] = xi[...]
    xc[64:72] = jnp.where(row_core == c, factors, 0.0).astype(BF)

    barrier = pltpu.get_barrier_semaphore()
    partners = [dev(c=1 - c), dev(a=1 - a), dev(a=1 - a, c=1 - c), dev(y=yd[1]), dev(y=yd[7])]
    partners += [dev(h=hd[1]), dev(h=hd[3]), dev(x=xd[1]), dev(x=xd[3]), dev(x=xd[2])]
    for to in partners:
        pl.semaphore_signal(barrier, inc=1, device_id=to, device_id_type=MESH)
    pl.semaphore_wait(barrier, len(partners))

    x0_recv = rsem.at[new_recv()]
    x0_send = send_sem("x0")

    def x0_other():
        return pltpu.make_async_remote_copy(
            src_ref=xc, dst_ref=xk.at[1 - c, m], send_sem=x0_send, recv_sem=x0_recv,
            device_id=dev(a=1 - a, c=1 - c), device_id_type=MESH,
        )

    def st_x0():
        @pl.when(c == a)
        def _():
            pltpu.make_async_copy(xc, xk.at[c, m], x0_recv).start()

        @pl.when(c != a)
        def _():
            x0_other().start()

        state["x0"] = [(xk.at[c, m], x0_recv)]

    own_recv = new_recv(2)

    def neighbours(slot, half):
        for table, to in ((UP, 1), (DOWN, 7)):
            dst = table.get(slot)
            if dst is None or (dst == 7 and half != (0 if table is UP else 1)):
                continue
            yield dst, dev(y=yd[to])

    def st_g0():
        for dst, to in neighbours(0, 0):
            state["ring", dst, 0] = [push("ring", g, gk.at[dst, a], to, gk.at[dst, a])]
        pltpu.make_async_copy(g, gk.at[0, a], rsem.at[own_recv]).start()
        pltpu.make_async_copy(q, qk.at[a, y], rsem.at[own_recv + 1]).start()
        state["own"] = [(gk.at[0, a], rsem.at[own_recv])]
        state["q", 0] = [(qk.at[a, y], rsem.at[own_recv + 1])]
        state["ring", 0, 1] = [push("gz0", g, gk.at[0, a], dev(a=1 - a), gk.at[0, 1 - a])]
        state["q", 0].append(push("qz0", q, qk.at[a, y], dev(a=1 - a), qk.at[1 - a, y]))

    def st_h1():
        wait("x0")
        mine = xk.at[c, m]
        for d in (1, 3):
            state["h", d] = [
                push("h1", mine, mine, dev(h=hd[d]), xk.at[c, x * NH + hd[NH - d]])
            ]

    def st_h2():
        far = x * NH + hd[2]
        recv = rsem.at[new_recv()]
        for d, rows in ((1, pl.ds(0, 40)), (3, pl.ds(40, 32))):
            wait(("h", d))
            part = xk.at[c, x * NH + hd[NH - d], rows]
            push("h2", part, part, dev(h=hd[d]), None, recv)
        state["h2"] = [(xk.at[c, far], recv)]

    def x_rows(at, rows=None):
        return pl.ds(at * NH, NH) if rows is None else pl.ds(at * NH + 2 * rows, 2)

    def to_core(rows):
        part = xk.at[c, rows]
        return push("xc", part, part, dev(c=1 - c), xk.at[1 - c, rows])

    def st_h3():
        wait("h2")
        mine = xk.at[c, x_rows(x)]
        for d in (1, 3):
            state["x", d] = [
                push("h3", mine, mine, dev(x=xd[d]), xk.at[c, x_rows(xd[NX - d])])
            ]
        state["xc", 0] = [to_core(x_rows(x))]

    def st_xs1():
        recv = rsem.at[new_recv()]
        for i, d in enumerate((1, 3)):
            wait(("x", d))
            part = xk.at[c, x_rows(xd[NX - d], i)]
            push("x2", part, part, dev(x=xd[d]), None, recv)
        state["x2"] = [(xk.at[c, x_rows(xd[2])], recv)]
        for d in (1, 3):
            state["xc", d] = [to_core(x_rows(xd[d]))]

    def x_piece(at):
        total = None
        for fb in range(2):
            rows = xk[fb, x_rows(at)].reshape(NH * 72, 512)
            part = jnp.dot(rows, bix[fb], preferred_element_type=F32)
            total = part if total is None else total + part
        sx[x_rows(at)] = total.astype(BF).reshape(NH, 72, 256)

    def st_bi():
        load_bi.wait()
        state["bi"] = [push("bi", bix.at[a], bix.at[a], dev(a=1 - a), bix.at[1 - a])]

    def st_xs2():
        wait("bi")
        for d in (0, 1, 3):
            wait(("xc", d))
            x_piece(xd[d])

    def st_xs3():
        wait("x2")
        state["xc", 2] = [to_core(x_rows(xd[2]))]

    def st_xm():
        wait(("xc", 2))
        x_piece(xd[2])

    def pair(at):
        return pl.ds(2 * at, 2)

    def st_xy():
        recv = rsem.at[new_recv()]
        for d in (1, 7, 2, 6, 3, 5, 4):
            push("xy", sx.at[pair(yd[d])], ryx.at[d - 1], dev(y=yd[d]), None, recv)
        state["xy"] = [(ryx, recv)]

    def st_xo():
        wait("xy")
        total = sx[pair(y)].astype(F32)
        for d in range(7):
            total += ryx[d].astype(F32)
        rx[a, pair(y)] = total.astype(BF)
        mine = rx.at[a, pair(y)]
        for d in (1, 7, 2, 6, 3, 5, 4):
            landing = rx.at[a, pair(yd[NY - d])]
            state["xo", d] = [push("xo", mine, mine, dev(y=yd[d]), landing)]
        recv = rsem.at[new_recv()]
        state["xz"] = [(rx.at[1 - a], recv)]
        push("xz", mine, mine, dev(a=1 - a), None, recv)

    def st_xz(ds):
        recv = state["xz"][0][1]
        for d in ds:
            wait(("xo", d))
            part = rx.at[a, pair(yd[NY - d])]
            push("xz", part, part, dev(a=1 - a), None, recv)

    def st_xf():
        wait("xz")
        for n in range(2):
            for s in range(8):
                shard = n * NY + wrap(y + OFFSETS[s], NY)
                for half in range(2):
                    at = s * 128 + half * 64
                    xf[n, at : at + 64] = rx[half, shard, 0:64]

    def st_bt():
        eye = (
            lax.broadcasted_iota(jnp.int32, (128, 128), 0)
            == lax.broadcasted_iota(jnp.int32, (128, 128), 1)
        ).astype(F32).astype(BF)
        load_b.wait()
        for j in range(7):
            cols = slice(j * 128, (j + 1) * 128)
            block = lax.dot_general(eye, bv[:, cols], NT, preferred_element_type=F32)
            bt[cols, :] = block.astype(BF)

    def st_ring(half, slots):
        n = a if half == 0 else 1 - a
        for slot in slots:
            wait(("ring", slot, half))
            for dst, to in neighbours(slot, half):
                state["ring", dst, half] = [
                    push("ring", gk.at[slot, n], gk.at[dst, n], to, gk.at[dst, n])
                ]

    def st_q(slots):
        for slot in slots:
            wait(("q", slot))
            mine = qk.at[:, wrap(y + OFFSETS[slot], NY)]
            for dst, to in neighbours(slot, 0):
                landing = qk.at[:, wrap(y + OFFSETS[dst], NY)]
                state["q", dst] = [push("q", mine, mine, to, landing)]

    def product(rows, s0, ns):
        def body(i, _):
            left = bt[pl.ds(pl.multiple_of(i * 224, 8), 224), :]
            terms = lax.dot_general(left, rows, NT, preferred_element_type=F32)
            for k in range(2 * ns):
                tile = terms[:, k * 128 : (k + 1) * 128].reshape(NH, 56, 128)
                if k < ns:
                    pf[s0 + k, pl.ds(i * NH, NH)] = tile
                else:
                    ps[s0 + k - ns, pl.ds(i * NH, NH)] = tile.astype(BF)
            return 0

        lax.fori_loop(0, NX, body, 0)
        landing = pr.at[pl.ds(s0, ns)]
        state[s0, "sum"] = [push("sum", ps.at[pl.ds(s0, ns)], landing, dev(c=1 - c), landing)]

    def st_bx(k):
        s0, ns = spans(k)
        wait((s0, "sum"))
        lane_core = lax.broadcasted_iota(jnp.int32, (16, 56, 128), 2) // 64
        for s in range(s0, s0 + ns):
            total = pf[s] + pr[s].astype(F32)
            if k == "q":
                total = jnp.where(lane_core == c, total, 0.0)
            pt[s] = total.astype(BF)
        slots = pl.ds(s0, ns)
        state[s0, "far"] = []
        for i, d in enumerate((1, 3)):
            landing = rf.at[i, slots]
            state[s0, "far"].append(
                push("far", pt.at[slots, rows_of(xd[2], i)], landing, dev(x=xd[d]), landing)
            )
        recv = rsem.at[new_recv()]
        state[s0, "x"] = [(r1.at[:, slots], recv)]
        for i, d in enumerate((1, 3)):
            landing = r1.at[i, slots, pl.ds(2 - 2 * i, 2)]
            push("x", pt.at[slots, rows_of(xd[d], 1 - i)], landing, dev(x=xd[d]), None, recv)

    def spans(k):
        return (QSLOT, 1) if k == "q" else CHUNKS[int(k)]

    def rows_of(at, half):
        return pl.ds(at * NH + 2 * half, 2)

    def st_by(k):
        s0, ns = spans(k)
        slots = pl.ds(s0, ns)
        for i, d in enumerate((1, 3)):
            arrival(*state[s0, "far"][i]).wait()
            for s in range(s0, s0 + ns):
                total = pt[s, rows_of(xd[d], i)].astype(F32) + rf[i, s].astype(F32)
                pa[i, s] = total.astype(BF)
            landing = r1.at[i, slots, pl.ds(2 * i, 2)]
            push("by", pa.at[i, slots], landing, dev(x=xd[d]), None, state[s0, "x"][0][1])
        del state[s0, "far"]

    def st_b1(k):
        s0, ns = spans(k)
        if k == "q":
            rows = qk[...].astype(F32).reshape(128, 896).astype(BF)
            rows = jnp.concatenate([rows, rows], axis=0)
        else:
            if k == "0":
                wait("own")
            rows = [gk[s0 : s0 + ns, n].reshape(ns * 128, 896) for n in (c, 1 - c)]
            rows = jnp.concatenate(rows, axis=0)
        product(rows, s0, ns)

    def st_b2(k):
        s0, ns = spans(k)
        wait((s0, "x"))
        for s in range(s0, s0 + ns):
            total = pt[s, pl.ds(x * NH, NH)].astype(F32)
            for d in range(2):
                total += r1[d, s].astype(F32)
            s1[s] = total.astype(BF)
        recv = rsem.at[new_recv()]
        slots = pl.ds(s0, ns)
        for d in (1, 3, 2):
            push("z", s1.at[slots, hd[d]], r2.at[d - 1, slots], dev(h=hd[d]), None, recv)
        state[s0, "z"] = [(r2.at[:, slots], recv)]

    def st_b3(k):
        s0, ns = spans(k)
        wait((s0, "z"))
        for s in range(s0, s0 + ns):
            total = s1[s, h].astype(F32)
            for d in range(3):
                total += r2[d, s].astype(F32)
            rg[c, s, m] = total.astype(BF)
        mine = rg.at[c, pl.ds(s0, ns), m]
        recv = rsem.at[new_recv()]
        for d in (1, 3, 2):
            push("gz", mine, mine, dev(h=hd[d]), None, recv)
        state[s0, "gz"] = [(r2.at[:, pl.ds(s0, ns)], recv)]

    def st_c2(k):
        s0, ns = spans(k)
        wait((s0, "gz"))
        mine = rg.at[c, pl.ds(s0, ns), pl.ds(x * NH, NH)]
        state[s0, "gx"] = [
            push("gx", mine, mine, dev(x=xd[d]), rg.at[c, pl.ds(s0, ns), pl.ds(xd[NX - d] * NH, NH)])
            for d in (1, 3)
        ]

    def st_cy(k):
        s0, ns = spans(k)
        slots = pl.ds(s0, ns)
        near = state.pop((s0, "gx"))
        recv = rsem.at[new_recv()]
        for i, d in enumerate((1, 3)):
            arrival(*near[i]).wait()
            part = rg.at[c, slots, rows_of(xd[NX - d], i)]
            push("cy", part, part, dev(x=xd[d]), None, recv)
        state[s0, "gx"] = [(rg.at[c, slots, pl.ds(xd[2] * NH, NH)], recv)]

    def out_copy(core, slots):
        pltpu.make_async_copy(
            rg.at[core, slots], rg_out.at[core, slots], rsem.at[out_recv]
        ).start()

    def st_c3(k):
        s0, ns = spans(k)
        slots = pl.ds(s0, ns)
        wait((s0, "gx"))
        mine = rg.at[c, slots]
        state[s0, "core"] = [push("core", mine, mine, dev(c=1 - c), rg.at[1 - c, slots])]
        out_copy(c, slots)

    def st_c4(k):
        s0, ns = spans(k)
        wait((s0, "core"))
        out_copy(1 - c, pl.ds(s0, ns))

    def st_fin():
        right = rx[0, :, 64:72].astype(F32) + rx[1, :, 64:72].astype(F32)
        right = right.reshape(128, 256)
        row_query = lax.broadcasted_iota(jnp.int32, (128, 256), 0) // 32
        for k in range(4):
            block = jnp.where(row_query == k, right, 0.0).astype(BF)
            right_v[:, k * 256 : (k + 1) * 256] = block
        for src, dst in ((xf, xf_out), (right_v, right_out)):
            outs.append(pltpu.make_async_copy(src, dst, rsem.at[out_recv + 1 + len(outs)]))
            outs[-1].start()

    plain = {
        "x0": st_x0, "g0": st_g0, "h1": st_h1, "h2": st_h2, "h3": st_h3, "xs1": st_xs1,
        "bi": st_bi, "xs2": st_xs2, "xs3": st_xs3, "xm": st_xm, "xy": st_xy, "xo": st_xo,
        "xf": st_xf, "bt": st_bt, "fin": st_fin,
    }
    keyed = {"b1": st_b1, "bx": st_bx, "by": st_by, "b2": st_b2, "b3": st_b3,
             "c2": st_c2, "cy": st_cy, "c3": st_c3, "c4": st_c4}
    for name in ORDER:
        with jax.named_scope(name):
            if name in plain:
                plain[name]()
            elif name.startswith("xz"):
                st_xz([int(v) for v in name[2:]])
            elif name.startswith("r"):
                for half in {"ra": (0,), "rb": (1,)}.get(name[:2], (0, 1)):
                    st_ring(half, [int(v) for v in name if v.isdigit()])
            elif name.startswith("q"):
                st_q([int(v) for v in name[1:]])
            else:
                keyed[name[:2]](name[3:])
    assert not state, state

    with jax.named_scope("outw"):
        pltpu.make_async_copy(rg, rg_out, rsem.at[out_recv]).wait()
        for copy in outs:
            copy.wait()

    @pl.when(c != a)
    def _():
        x0_other().wait_send()

    with jax.named_scope("sentw"):
        totals = {
            "ring": gk.at[1:8], "gz0": gk.at[0, 0], "q": qk.at[:, 0:7], "qz0": qk.at[0, 0],
            "h1": xk.at[0, 0:2], "h2": xk.at[0, 0], "h3": xk.at[0, 0:8], "x2": xk.at[0, 0:4],
            "xc": xk.at[0], "bi": bix.at[0], "xy": ryx, "xo": ryx, "xz": rx.at[0],
            "sum": ps, "far": rf, "x": rf, "by": rf, "z": r2, "gz": r2, "gx": r1, "cy": rf,
            "core": rg.at[0],
        }
        for kind, ref in totals.items():
            arrival(ref, ssem.at[sends[kind]]).wait()
        assert set(sends) == set(totals) | {"x0"}


def last_kernel(rg, xf, right, damp, eig, pre):
    squares = None
    for n in range(2):
        left = jnp.concatenate([rg[n, s].reshape(224, 128) for s in range(8)], axis=1)
        rotated = jnp.dot(left, xf[n], preferred_element_type=F32)
        square = rotated * rotated
        squares = square if squares is None else squares + square
    values = squares * (1.0 / 2048.0)
    eig[...] = values
    scale = 1.0 / (values + damp[0])
    left = (rg[0, QSLOT] + rg[1, QSLOT]).reshape(224, 128)
    products = jnp.dot(left, right[...], preferred_element_type=F32)
    for k in range(4):
        pre[k] = (products[:, k * 256 : (k + 1) * 256] * scale).astype(BF)


def shards(out_grads, inputs, out_basis, in_basis, query_out, query_in, damping):
    vmem = pl.BlockSpec(memory_space=pltpu.VMEM)
    hbm = pl.BlockSpec(memory_space=pl.ANY)
    rg, xf, right = pl.pallas_call(
        kernel,
        out_shape=(
            jax.ShapeDtypeStruct((2, 9, 16, 56, 128), BF),
            jax.ShapeDtypeStruct((2, 1024, 256), BF),
            jax.ShapeDtypeStruct((128, 1024), BF),
        ),
        in_specs=[hbm, hbm, hbm, vmem, vmem, hbm],
        out_specs=(hbm, hbm, hbm),
        scratch_shapes=[
            pltpu.VMEM((8, 2, 128, 896), BF),
            pltpu.VMEM((2, 8, 8, 896), BF),
            pltpu.VMEM((896, 896), BF),
            pltpu.VMEM((896, 896), BF),
            pltpu.VMEM((2, 512, 256), BF),
            pltpu.VMEM((9, 16, 56, 128), F32),
            pltpu.VMEM((9, 16, 56, 128), BF),
            pltpu.VMEM((9, 16, 56, 128), BF),
            pltpu.VMEM((9, 16, 56, 128), BF),
            pltpu.VMEM((2, 9, 2, 56, 128), BF),
            pltpu.VMEM((2, 9, 2, 56, 128), BF),
            pltpu.VMEM((2, 9, 4, 56, 128), BF),
            pltpu.VMEM((9, 4, 56, 128), BF),
            pltpu.VMEM((3, 9, 56, 128), BF),
            pltpu.VMEM((2, 9, 16, 56, 128), BF),
            pltpu.VMEM((72, 512), BF),
            pltpu.VMEM((2, 16, 72, 512), BF),
            pltpu.VMEM((16, 72, 256), BF),
            pltpu.VMEM((7, 2, 72, 256), BF),
            pltpu.VMEM((2, 16, 72, 256), BF),
            pltpu.VMEM((2, 1024, 256), BF),
            pltpu.VMEM((128, 1024), BF),
            pltpu.SemaphoreType.DMA((N_SEND,)),
            pltpu.SemaphoreType.DMA((N_RECV,)),
        ],
        compiler_params=pltpu.CompilerParams(
            collective_id=0, has_side_effects=True, vmem_limit_bytes=60 * 1024 * 1024
        ),
    )(out_grads, query_out, out_basis, inputs, query_in, in_basis)
    return pl.pallas_call(
        last_kernel,
        grid=(NX,),
        out_shape=(
            jax.ShapeDtypeStruct((896, 256), F32),
            jax.ShapeDtypeStruct((4, 896, 256), BF),
        ),
        in_specs=[
            pl.BlockSpec((2, 9, NH, 56, 128), lambda i: (0, 0, i, 0, 0)),
            pl.BlockSpec((2, 1024, 256), lambda i: (0, 0, 0)),
            pl.BlockSpec((128, 1024), lambda i: (0, 0)),
            pl.BlockSpec(memory_space=pltpu.SMEM),
        ],
        out_specs=(
            pl.BlockSpec((224, 256), lambda i: (i, 0)),
            pl.BlockSpec((4, 224, 256), lambda i: (0, i, 0)),
        ),
        compiler_params=pltpu.CompilerParams(vmem_limit_bytes=60 * 1024 * 1024),
    )(rg, xf, right, damping)


def solution(mesh):
    placed = (
        P("dp", "mp"),
        P("mp", "dp"),
        P("mp", "dp"),
        P("dp", "mp"),
        P("dp", "mp"),
        P("mp", "dp"),
        P(),
    )
    return jax.shard_map(
        shards,
        mesh=mesh,
        in_specs=placed,
        out_specs=(P("dp", "mp"), P(None, "dp", "mp")),
        check_vma=False,
    )
```

time: 443 us -> 102 us (0.23)
  the two profiles are of different devices: /device:TPU:2 before, /device:TPU:1 now
where the time goes in v2:
time: 102 us
  Pallas kernels  100 us (98%)
  between operations  1.29 us (1%)
    pallas_call x1, Pallas kernels, shards(): pl.pallas_call(kernel, out_shape=(jax.ShapeDtypeStruct((2, 9, 16, 56, 128...  95 us
    pallas_call x1, Pallas kernels, shards(): pl.pallas_call(last_kernel, grid=(NX,), out_shape=(jax.ShapeDtypeStruct((...  5.49 us

profile of v2, /device:TPU:1, one launch (start us, length us, event | category | flops | bytes accessed | tf_op | source)
XLA Modules:
  0.0 101.8 jit_solution(13323883027000679292)
XLA Ops:
  1.3 95.0 %shard_map.86 = (bf16[2,9,16,56,128]{4,3,2,1,0:T(8,128)(2,1)}, bf16[2,1024,256]{2,1,0:T(8,128)(2,1)}, bf16[128,1024]{1,0:T(8,128)(2,1)}) custom-call(bf16[128,896]{1,0:T(8,128)(2,1)} %g.1, bf16[8,896]{1,0:T(8,128)(2,1)} %q.1, bf16[896,896]{1,0:T(8,128)(2,1)} %b.1, bf16[64,512]{1,0:T(8,128)(2,1)} %xi.1, bf16[4,512]{1,0:T(4,128)(2,1)} %qi.1, bf16[512,256]{1,0:T(8,128)(2,1)} %bi.1), custom_call_target="tpu_custom_call" | custom-call | tf_op jit(solution)/shard_map/pallas_call | solution.py:485
  96.3 5.5 %shard_map.87 = (f32[896,256]{1,0:T(8,128)}, bf16[4,896,256]{2,1,0:T(8,128)(2,1)}) custom-call(bf16[2,9,16,56,128]{4,3,2,1,0:T(8,128)(2,1)} %get-tuple-element.5.rg, bf16[2,1024,256]{2,1,0:T(8,128)(2,1)} %get-tuple-element.6.xf, bf16[128,1024]{1,0:T(8,128)(2,1)} %get-tuple-element.7.right, f32[1]{0:T(128)S(6)} %copy.9.damp), custom_call_target="tpu_custom_call" | custom-call | tf_op jit(solution)/shard_map/pallas_call | solution.py:524

commit v3 on v2

--- a/solution.py
+++ b/solution.py
@@ -22,9 +22,9 @@
     "x0", "g0", "bt", "rb0", "h1", "q0", "ra12", "b1_0", "h2", "rb12", "q12", "h3", "bi", "bx_0", "b1_1",
     "ra34", "bx_1", "xs1", "rb34", "q34", "by_0", "b1_2", "by_1", "xs2", "xs3", "b2_0", "bx_2", "ra56", "b2_1",
     "rb56", "q56", "xm", "b1_3", "b3_0", "by_2", "b3_1", "bx_3", "r7", "xy", "b1_4", "q7", "b1_q", "c2_0",
-    "b2_2", "by_3", "bx_4", "bx_q", "c2_1", "cy_0", "b3_2", "b2_3", "by_4", "by_q", "c3_0", "cy_1", "c2_2",
-    "b2_4", "b2_q", "xo", "b3_3", "c3_1", "b3_4", "b3_q", "cy_2", "xz17", "c2_3", "xz26", "c2_4", "c2_q",
-    "c3_2", "cy_3", "xz354", "cy_4", "cy_q", "c3_3", "c3_4", "c3_q", "c4_0", "c4_1", "c4_2", "xf", "fin",
+    "b2_2", "by_3", "bx_4", "bx_q", "c2_1", "b3_2", "b2_3", "by_4", "by_q", "cy_0", "cy_1", "c2_2", "b2_4",
+    "b2_q", "xo", "b3_3", "c3_0", "b3_4", "b3_q", "cy_2", "xz17", "c2_3", "c2_4", "c2_q", "xz26", "c3_1",
+    "c3_2", "cy_3", "cy_4", "cy_q", "xz354", "c3_3", "c3_4", "c3_q", "c4_0", "c4_1", "c4_2", "xf", "fin",
     "c4_3", "c4_4", "c4_q",
 )
 
@@ -363,8 +363,8 @@
             total = s1[s, h].astype(F32)
             for d in range(3):
                 total += r2[d, s].astype(F32)
-            rg[c, s, m] = total.astype(BF)
-        mine = rg.at[c, pl.ds(s0, ns), m]
+            rg[s, m] = total.astype(BF)
+        mine = rg.at[pl.ds(s0, ns), m]
         recv = rsem.at[new_recv()]
         for d in (1, 3, 2):
             push("gz", mine, mine, dev(h=hd[d]), None, recv)
@@ -373,9 +373,9 @@
     def st_c2(k):
         s0, ns = spans(k)
         wait((s0, "gz"))
-        mine = rg.at[c, pl.ds(s0, ns), pl.ds(x * NH, NH)]
+        mine = rg.at[pl.ds(s0, ns), pl.ds(x * NH, NH)]
         state[s0, "gx"] = [
-            push("gx", mine, mine, dev(x=xd[d]), rg.at[c, pl.ds(s0, ns), pl.ds(xd[NX - d] * NH, NH)])
+            push("gx", mine, mine, dev(x=xd[d]), rg.at[pl.ds(s0, ns), pl.ds(xd[NX - d] * NH, NH)])
             for d in (1, 3)
         ]
 
@@ -386,27 +386,23 @@
         recv = rsem.at[new_recv()]
         for i, d in enumerate((1, 3)):
             arrival(*near[i]).wait()
-            part = rg.at[c, slots, rows_of(xd[NX - d], i)]
+            part = rg.at[slots, rows_of(xd[NX - d], i)]
             push("cy", part, part, dev(x=xd[d]), None, recv)
-        state[s0, "gx"] = [(rg.at[c, slots, pl.ds(xd[2] * NH, NH)], recv)]
-
-    def out_copy(core, slots):
-        pltpu.make_async_copy(
-            rg.at[core, slots], rg_out.at[core, slots], rsem.at[out_recv]
-        ).start()
+        state[s0, "gx"] = [(rg.at[slots, pl.ds(xd[2] * NH, NH)], recv)]
 
     def st_c3(k):
         s0, ns = spans(k)
         slots = pl.ds(s0, ns)
         wait((s0, "gx"))
-        mine = rg.at[c, slots]
-        state[s0, "core"] = [push("core", mine, mine, dev(c=1 - c), rg.at[1 - c, slots])]
-        out_copy(c, slots)
+        mine = rg.at[slots]
+        state[s0, "core"] = [
+            push("core", mine, rg_out.at[c, slots], dev(c=1 - c), rg_out.at[1 - c, slots])
+        ]
+        pltpu.make_async_copy(mine, rg_out.at[c, slots], rsem.at[out_recv]).start()
 
     def st_c4(k):
         s0, ns = spans(k)
         wait((s0, "core"))
-        out_copy(1 - c, pl.ds(s0, ns))
 
     def st_fin():
         right = rx[0, :, 64:72].astype(F32) + rx[1, :, 64:72].astype(F32)
@@ -442,7 +438,7 @@
     assert not state, state
 
     with jax.named_scope("outw"):
-        pltpu.make_async_copy(rg, rg_out, rsem.at[out_recv]).wait()
+        pltpu.make_async_copy(rg, rg_out.at[c], rsem.at[out_recv]).wait()
         for copy in outs:
             copy.wait()
 
@@ -456,7 +452,7 @@
             "h1": xk.at[0, 0:2], "h2": xk.at[0, 0], "h3": xk.at[0, 0:8], "x2": xk.at[0, 0:4],
             "xc": xk.at[0], "bi": bix.at[0], "xy": ryx, "xo": ryx, "xz": rx.at[0],
             "sum": ps, "far": rf, "x": rf, "by": rf, "z": r2, "gz": r2, "gx": r1, "cy": rf,
-            "core": rg.at[0],
+            "core": rg,
         }
         for kind, ref in totals.items():
             arrival(ref, ssem.at[sends[kind]]).wait()
@@ -466,14 +462,14 @@
 def last_kernel(rg, xf, right, damp, eig, pre):
     squares = None
     for n in range(2):
-        left = jnp.concatenate([rg[n, s].reshape(224, 128) for s in range(8)], axis=1)
+        left = jnp.concatenate([rg[n, s].reshape(448, 128) for s in range(8)], axis=1)
         rotated = jnp.dot(left, xf[n], preferred_element_type=F32)
         square = rotated * rotated
         squares = square if squares is None else squares + square
     values = squares * (1.0 / 2048.0)
     eig[...] = values
     scale = 1.0 / (values + damp[0])
-    left = (rg[0, QSLOT] + rg[1, QSLOT]).reshape(224, 128)
+    left = (rg[0, QSLOT] + rg[1, QSLOT]).reshape(448, 128)
     products = jnp.dot(left, right[...], preferred_element_type=F32)
     for k in range(4):
         pre[k] = (products[:, k * 256 : (k + 1) * 256] * scale).astype(BF)
@@ -506,7 +502,7 @@
             pltpu.VMEM((2, 9, 4, 56, 128), BF),
             pltpu.VMEM((9, 4, 56, 128), BF),
             pltpu.VMEM((3, 9, 56, 128), BF),
-            pltpu.VMEM((2, 9, 16, 56, 128), BF),
+            pltpu.VMEM((9, 16, 56, 128), BF),
             pltpu.VMEM((72, 512), BF),
             pltpu.VMEM((2, 16, 72, 512), BF),
             pltpu.VMEM((16, 72, 256), BF),
@@ -523,20 +519,20 @@
     )(out_grads, query_out, out_basis, inputs, query_in, in_basis)
     return pl.pallas_call(
         last_kernel,
-        grid=(NX,),
+        grid=(2,),
         out_shape=(
             jax.ShapeDtypeStruct((896, 256), F32),
             jax.ShapeDtypeStruct((4, 896, 256), BF),
         ),
         in_specs=[
-            pl.BlockSpec((2, 9, NH, 56, 128), lambda i: (0, 0, i, 0, 0)),
+            pl.BlockSpec((2, 9, 8, 56, 128), lambda i: (0, 0, i, 0, 0)),
             pl.BlockSpec((2, 1024, 256), lambda i: (0, 0, 0)),
             pl.BlockSpec((128, 1024), lambda i: (0, 0)),
             pl.BlockSpec(memory_space=pltpu.SMEM),
         ],
         out_specs=(
-            pl.BlockSpec((224, 256), lambda i: (i, 0)),
-            pl.BlockSpec((4, 224, 256), lambda i: (0, i, 0)),
+            pl.BlockSpec((448, 256), lambda i: (i, 0)),
+            pl.BlockSpec((4, 448, 256), lambda i: (0, i, 0)),
         ),
         compiler_params=pltpu.CompilerParams(vmem_limit_bytes=60 * 1024 * 1024),
     )(rg, xf, right, damping)

time: 102 us -> 100 us (0.980)
  Pallas kernels: 100 us -> 98 us
    pallas_call x1, Pallas kernels: 95 us -> 93.4 us  [shards(): pl.pallas_call(kernel, out_shape=(jax.ShapeDtypeStruct((2, 9, 16, 56, 128...]
where the time goes in v3:
time: 100 us; the launch traced here: 99.3 us
  Pallas kernels  98 us (98%)
  between operations  1.29 us (1%)
    pallas_call x1, Pallas kernels, shards(): pl.pallas_call(kernel, out_shape=(jax.ShapeDtypeStruct((2, 9, 16, 56, 128...  93.4 us
    pallas_call x1, Pallas kernels, shards(): pl.pallas_call(last_kernel, grid=(2,), out_shape=(jax.ShapeDtypeStruct((8...  4.63 us

profile of v3, /device:TPU:1, one launch (start us, length us, event | category | flops | bytes accessed | tf_op | source)
XLA Modules:
  0.0 99.3 jit_solution(18325978413019140596)
XLA Ops:
  1.3 93.4 %shard_map.86 = (bf16[2,9,16,56,128]{4,3,2,1,0:T(8,128)(2,1)}, bf16[2,1024,256]{2,1,0:T(8,128)(2,1)}, bf16[128,1024]{1,0:T(8,128)(2,1)}) custom-call(bf16[128,896]{1,0:T(8,128)(2,1)} %g.1, bf16[8,896]{1,0:T(8,128)(2,1)} %q.1, bf16[896,896]{1,0:T(8,128)(2,1)} %b.1, bf16[64,512]{1,0:T(8,128)(2,1)} %xi.1, bf16[4,512]{1,0:T(4,128)(2,1)} %qi.1, bf16[512,256]{1,0:T(8,128)(2,1)} %bi.1), custom_call_target="tpu_custom_call" | custom-call | tf_op jit(solution)/shard_map/pallas_call | solution.py:481
  94.7 4.6 %shard_map.87 = (f32[896,256]{1,0:T(8,128)}, bf16[4,896,256]{2,1,0:T(8,128)(2,1)}) custom-call(bf16[2,9,16,56,128]{4,3,2,1,0:T(8,128)(2,1)} %get-tuple-element.5.rg, bf16[2,1024,256]{2,1,0:T(8,128)(2,1)} %get-tuple-element.6.xf, bf16[128,1024]{1,0:T(8,128)(2,1)} %get-tuple-element.7.right, f32[1]{0:T(128)S(6)} %copy.9.damp), custom_call_target="tpu_custom_call" | custom-call | tf_op jit(solution)/shard_map/pallas_call | solution.py:520
